TPU v7x, 32 devices: a whole 2x2x4 slice. The times are simulated.
32 devices in a mesh: dap: 8 (over y, x, core), seq: 4 (over z).
Axes of the slice: x: 2, y: 2, z: 4, core: 2. Of those that a mesh axis runs over, the one named last changes fastest.
Arguments:
- homolog_tensor: bfloat16 [8, 32, 256], P('dap', 'seq'), may hold values from -6 to 6
- pair_features: bfloat16 [32, 32, 128], P('seq', 'dap'), may hold values from -6 to 6
- entry_real_mask: int32 [8, 32], P('dap', 'seq'), may hold values 0 or 1
- chain_ids: int32 [32], replicated, may hold values from 0 to 3, never falling along the last dimension, each value on 1 to 16 neighbouring positions
- horizontal_matrices: bfloat16 [256, 1024], replicated, may hold values from -0.375 to 0.375
- horizontal_projector: bfloat16 [256, 256], replicated, may hold values from -0.375 to 0.375
- bias_proj: float32 [128, 8], replicated, may hold values from -35.35534 to 35.35534
- chain_bias: float32 [2, 8], replicated, may hold values from -4 to 4
- column_proj: bfloat16 [256, 1024], replicated, may hold values from -12.5 to 12.5
- vertical_projector: bfloat16 [256, 256], replicated, may hold values from -0.375 to 0.375
- expansion_matrix: bfloat16 [256, 1024], replicated, may hold values from -0.375 to 0.375
- contraction_matrix: bfloat16 [1024, 256], replicated, may hold values from -0.1875 to 0.1875
Outputs:
- updated: bfloat16 [8, 32, 256], P('dap', 'seq')
Inputs may be any that keep to these rules, and one draw needn't show every extreme that they name: `chain_ids`: chain numbers never fall along the residues.
All inputs are finite; a program needn't handle non-finite values. No bound on the sum of `entry_real_mask` on one device may be relied on, other than what follows from the above.
Results may differ from a plain program's by a relative error of at most 0.013.
The roundings to bfloat16 on the way count: a program that leaves them out, or rounds other values in their place, can miss the bound.
Values may be sent and summed in bfloat16 or wider, within the bound.
No kernel may reach another device: no remote copies, remote signals or barrier semaphores. Data moves between devices by JAX's collectives and lax.ppermute only.
A program may use at most 64 MiB of HBM per device.

v0:
```python
import jax
import jax.numpy as jnp
from jax import lax
from jax.sharding import PartitionSpec as P

HEAD_TOTAL = 8
HEAD_DEPTH = 32
epsilon = 1e-05


def layer_norm(inputs):
    center = inputs - jnp.mean(inputs, axis=-1, keepdims=True)
    spread = jnp.mean(center * center, axis=-1, keepdims=True)
    return center * lax.rsqrt(spread + epsilon)


def attend(queries, key_part, value_part, keep_mask, bias_term):
    scores = jnp.einsum(
        "ihd,jhd->hij", queries, key_part, preferred_element_type=jnp.float32
    ) * HEAD_DEPTH ** (-0.5)
    if bias_term is not None:
        scores = scores + bias_term.astype(jnp.float32)
    scores = jnp.where(keep_mask[None, None, :] > 0, scores, -1000000000.0)
    weights = jax.nn.softmax(scores, axis=-1).astype(jnp.bfloat16)
    return jnp.einsum("hij,jhd->ihd", weights, value_part, preferred_element_type=jnp.float32)


def column_update(
    column, keep_column, column_proj, vertical_projector, expansion_matrix, contraction_matrix
):
    expanded_dimension = HEAD_TOTAL * HEAD_DEPTH
    standardized = layer_norm(column.astype(jnp.float32)).astype(jnp.bfloat16)
    projected = jnp.dot(standardized, column_proj, preferred_element_type=jnp.float32).astype(
        jnp.bfloat16
    )
    queries = projected[:, :expanded_dimension].reshape(-1, HEAD_TOTAL, HEAD_DEPTH)
    key_part = projected[:, expanded_dimension : 2 * expanded_dimension].reshape(
        -1, HEAD_TOTAL, HEAD_DEPTH
    )
    value_part = projected[:, 2 * expanded_dimension : 3 * expanded_dimension].reshape(
        -1, HEAD_TOTAL, HEAD_DEPTH
    )
    attended = attend(queries, key_part, value_part, keep_column, None).reshape(
        -1, expanded_dimension
    )
    sigmoid_scaled = (
        jax.nn.sigmoid(projected[:, 3 * expanded_dimension :].astype(jnp.float32)) * attended
    ).astype(jnp.bfloat16)
    mixed = column.astype(jnp.float32) + jnp.dot(
        sigmoid_scaled, vertical_projector, preferred_element_type=jnp.float32
    )
    inner = jnp.maximum(
        jnp.dot(
            layer_norm(mixed).astype(jnp.bfloat16),
            expansion_matrix,
            preferred_element_type=jnp.float32,
        ),
        0.0,
    ).astype(jnp.bfloat16)
    return (mixed + jnp.dot(inner, contraction_matrix, preferred_element_type=jnp.float32)).astype(
        jnp.bfloat16
    )


def body(
    homolog_tensor,
    pair_features,
    entry_real_mask,
    chain_ids,
    horizontal_matrices,
    horizontal_projector,
    bias_proj,
    chain_bias,
    column_proj,
    vertical_projector,
    expansion_matrix,
    contraction_matrix,
):
    row_count, local_residues, channels = homolog_tensor.shape
    expanded_dimension = HEAD_TOTAL * HEAD_DEPTH
    dap_count = lax.axis_size("dap")
    pair_rows, pair_columns, pair_width = pair_features.shape
    normed_pair = layer_norm(pair_features.astype(jnp.float32))
    projected_pair = jnp.einsum(
        "ijc,ch->hij", normed_pair, bias_proj, precision=lax.Precision.HIGHEST
    )
    row_chain = lax.dynamic_slice_in_dim(chain_ids, lax.axis_index("seq") * pair_rows, pair_rows)
    column_chain = lax.dynamic_slice_in_dim(
        chain_ids, lax.axis_index("dap") * pair_columns, pair_columns
    )
    same_chain = (row_chain[:, None] == column_chain[None, :]).astype(jnp.float32)
    chain_term = chain_bias[0][:, None, None] * same_chain + chain_bias[1][:, None, None] * (
        1.0 - same_chain
    )
    local_bias = (projected_pair + chain_term).astype(jnp.bfloat16)
    pair_bias = lax.all_gather(local_bias, "dap", axis=2, tiled=True)
    standardized = layer_norm(homolog_tensor.astype(jnp.float32)).astype(jnp.bfloat16)
    flat = standardized.reshape(-1, channels)
    keep_mask = entry_real_mask.astype(jnp.bfloat16)
    projected = (
        jnp.dot(flat, horizontal_matrices, preferred_element_type=jnp.float32)
        .astype(jnp.bfloat16)
        .reshape(row_count, local_residues, 4 * expanded_dimension)
    )
    queries = projected[..., :expanded_dimension]
    gating = projected[..., 3 * expanded_dimension :]
    key_values, keep_all = (
        lax.all_gather(
            projected[..., expanded_dimension : 3 * expanded_dimension], "seq", axis=1, tiled=True
        ),
        lax.all_gather(keep_mask, "seq", axis=1, tiled=True),
    )

    def one_row(inputs_row):
        row_queries, row_pairs, row_keep = inputs_row
        key_part = row_pairs[:, :expanded_dimension].reshape(-1, HEAD_TOTAL, HEAD_DEPTH)
        value_part = row_pairs[:, expanded_dimension:].reshape(-1, HEAD_TOTAL, HEAD_DEPTH)
        return attend(
            row_queries.reshape(local_residues, HEAD_TOTAL, HEAD_DEPTH),
            key_part,
            value_part,
            row_keep,
            pair_bias,
        ).reshape(local_residues, expanded_dimension)

    attended = lax.map(one_row, (queries, key_values, keep_all))
    sigmoid_scaled = (jax.nn.sigmoid(gating.astype(jnp.float32)) * attended).astype(jnp.bfloat16)
    row_result = jnp.dot(
        sigmoid_scaled.reshape(-1, expanded_dimension),
        horizontal_projector,
        preferred_element_type=jnp.float32,
    ).reshape(row_count, local_residues, channels)
    updated_rows = (homolog_tensor.astype(jnp.float32) + row_result).astype(jnp.bfloat16)
    per_device = local_residues // dap_count
    blocks = updated_rows.reshape(row_count, dap_count, per_device, channels)
    keep_blocks = keep_mask.reshape(row_count, dap_count, per_device)

    def single_column(inputs_col):
        return column_update(
            inputs_col[0],
            inputs_col[1],
            column_proj,
            vertical_projector,
            expansion_matrix,
            contraction_matrix,
        )

    column_block = lax.all_to_all(blocks, "dap", split_axis=1, concat_axis=0, tiled=True)
    column_keep = lax.all_to_all(keep_blocks, "dap", split_axis=1, concat_axis=0, tiled=True)
    inputs_col = (jnp.moveaxis(column_block[:, 0], 1, 0), jnp.moveaxis(column_keep[:, 0], 1, 0))
    output_list = lax.map(single_column, inputs_col)
    mixed = jnp.moveaxis(output_list, 0, 1)[:, None]
    returned = lax.all_to_all(mixed, "dap", split_axis=0, concat_axis=1, tiled=True)
    return returned.reshape(row_count, local_residues, channels)


def solution(mesh):
    placed = (
        P("dap", "seq", None),
        P("seq", "dap", None),
        P("dap", "seq"),
        P(),
        P(),
        P(),
        P(),
        P(),
        P(),
        P(),
        P(),
        P(),
    )
    return jax.shard_map(
        body, mesh=mesh, in_specs=placed, out_specs=P("dap", "seq", None), check_vma=False
    )
```

profile of v0, /device:TPU:0, one launch (start us, length us, event | category | flops | bytes accessed | tf_op | source)
XLA Modules:
  0.0 71.7 jit_solution(17577258312015481253)
XLA Ops:
  0.0 0.7 convert_bitcast_fusion.1
  0.7 0.7 copy.49
  1.4 5.2 %all-to-all-start.1 = ((bf16[1,8,1]{2,0,1:T(2,128)(2,1)}), bf16[1,8,1]{2,0,1:T(2,128)(2,1)S(1)}, u32[]{:S(2)}, u32[]{:S(2)}) async-start(bf16[1,8,1]{2,0,1:T(2,128)(2,1)} %copy.49), calls=%async_computation.1 | async-start | bytes 8192 | tf_op jit(solution)/shard_map/all_to_all | solution.py:149
  6.6 0.7 copy-done.12
  7.3 0.1 dynamic_slice.21
  7.3 0.1 dynamic_slice.20
  7.4 0.1 broadcast_subtract_fusion
  7.5 0.1 compare_convert_fusion
  7.6 0.5 copy-done.6
  8.0 0.1 convert_reduce_fusion.1
  8.1 0.2 fusion.38
  8.3 0.2 fusion.12
  8.6 0.6 copy-done.7
  9.2 0.7 copy-done.5
  9.9 0.1 convert_reduce_fusion
  10.0 0.2 fusion.24
  10.1 0.0 copy-start.9
  10.1 0.1 fusion.22
  10.2 0.6 copy-done.9
  10.8 0.7 copy-done.11
  11.5 0.1 fusion.13
  11.6 0.1 copy.43
  11.7 9.7 %all_gather.11 = bf16[8,8,32]{1,0,2:T(8,128)(2,1)S(1)} all-gather(bf16[8,8,4]{1,0,2:T(8,128)(2,1)S(1)} %copy.43), channel_id=1, replica_groups=mesh['dap'=8,'seq'=4] {'dap'}, dimensions={2}, use_global_device_ids=true | all-gather | bytes 4608 | tf_op jit(solution)/shard_map/all_gather | solution.py:96
  21.5 0.1 copy.44
  21.6 0.6 slice-done
  22.2 13.4 %all_gather.9 = bf16[1,32,512]{2,1,0:T(8,128)(2,1)S(1)} all-gather(bf16[1,8,512]{2,1,0:T(8,128)(2,1)S(1)} %slice-done), channel_id=1, replica_groups=mesh['dap'=8,'seq'=4] {'seq'}, dimensions={1}, use_global_device_ids=true | all-gather | bytes 40960 | tf_op jit(solution)/shard_map/all_gather | solution.py:108
  35.6 0.1 reshape.208
  35.7 0.6 slice-done.1
  36.2 0.1 reshape.207
  36.3 0.6 dynamic-slice
  37.6 0.2 dynamic-update-slice
  37.8 11.7 %all-reduce = bf16[32]{0:T(256)(128)(2,1)S(1)} all-reduce(bf16[32]{0:T(256)(128)(2,1)S(1)} %dynamic-update-slice), channel_id=1, replica_groups=mesh['dap'=8,'seq'=4] {'seq'}, use_global_device_ids=true, to_apply=%add | all-reduce | flops 32 | bytes 128
  49.5 0.1 fusion.8
  49.7 0.2 fusion.66
  49.9 0.1 reshape.206
  50.0 0.0 copy-start.3
  50.0 0.3 convolution_bitcast_fusion.1
  50.3 0.1 broadcast_in_dim.72
  50.3 0.5 copy-done.3
  50.9 0.1 copy-done.8
  51.0 0.1 fusion.19
  51.2 0.6 broadcast.220
  51.8 0.7 %reduce.5 = bf16[8,256]{1,0:T(8,128)(2,1)S(1)} reduce(bf16[8,1,1,256]{3,2,1,0:T(2,128)(2,1)S(1)} %bitcast.75, bf16[]{:T(256)} %broadcast.220), dimensions={1,2}, to_apply=%bitcast.73.reduce_sub_computation | reduce | bytes 8194
  52.5 0.6 reshape.228
  53.1 3.3 %all-to-all-start = ((bf16[8,2,128]{2,1,0:T(2,128)(2,1)}), bf16[8,2,128]{2,1,0:T(2,128)(2,1)S(1)}, u32[]{:S(2)}, u32[]{:S(2)}) async-start(bf16[8,2,128]{2,1,0:T(2,128)(2,1)} %reshape.228), calls=%async_computation | async-start | bytes 8192 | tf_op jit(solution)/shard_map/all_to_all | solution.py:148
  56.4 0.2 compare_reduce_fusion
  56.6 4.3 %all-to-all-done = bf16[8,2,128]{2,1,0:T(2,128)(2,1)S(1)} async-done(((bf16[8,2,128]{2,1,0:T(2,128)(2,1)}), bf16[8,2,128]{2,1,0:T(2,128)(2,1)S(1)}, u32[]{:S(2)}, u32[]{:S(2)}) %all-to-all-start) | async-done | bytes 4128 | tf_op jit(solution)/shard_map/all_to_all | solution.py:148
  61.0 0.1 convert_reduce_fusion.2
  61.1 0.2 fusion.40
  61.3 0.0 copy-start.4
  61.3 0.2 convolution_convert_fusion
  61.5 0.1 reshape.214
  61.6 0.1 reshape.215
  61.7 0.1 fusion.6
  61.8 0.2 fusion.67
  62.0 0.1 reshape.212
  62.1 0.2 convolution_bitcast_fusion
  62.3 0.1 reshape.216
  62.4 0.3 fusion.72
  62.7 0.2 multiply_reduce_fusion
  62.9 0.4 fusion.18
  63.3 0.7 reduce.6
  64.0 7.1 %all_to_all.12 = bf16[8,2,128]{2,1,0:T(2,128)(2,1)S(1)} all-to-all(bf16[8,2,128]{2,1,0:T(2,128)(2,1)S(1)} %reshape.230), channel_id=1, replica_groups=mesh['dap'=8,'seq'=4] {'dap'}, dimensions={0} | all-to-all | bytes 8192 | tf_op jit(solution)/shard_map/all_to_all | solution.py:153
  71.1 0.6 copy.83
  (39 shorter events, 0.2 us)
Async XLA Ops:
  0.0 8.3 %copy-start = (bf16[256,1024]{1,0:T(8,128)(2,1)S(1)}, bf16[256,1024]{1,0:T(8,128)(2,1)}, u32[]{:S(2)}) copy-start(bf16[256,1024]{1,0:T(8,128)(2,1)} %param.16) | copy-start | bytes 1572868
  1.4 51.7 %all-to-all-start.1 = ((bf16[1,8,1]{2,0,1:T(2,128)(2,1)}), bf16[1,8,1]{2,0,1:T(2,128)(2,1)S(1)}, u32[]{:S(2)}, u32[]{:S(2)}) async-start(bf16[1,8,1]{2,0,1:T(2,128)(2,1)} %copy.49), calls=%async_computation.1 | async-start | bytes 8192 | tf_op jit(solution)/shard_map/all_to_all | solution.py:149
  6.6 0.7 copy-start.12
  7.3 0.7 copy-start.6
  8.6 0.6 copy-start.7
  9.2 0.7 copy-start.5
  10.1 0.7 copy-start.9
  10.8 0.7 copy-start.11
  21.5 0.7 slice-start
  35.5 0.8 %copy-start.13 = (u32[32]{0:T(128)S(1)}, u32[32]{0:T(128)}, u32[]{:S(2)}) copy-start(u32[32]{0:T(128)} %constant.98) | copy-start | bytes 388
  35.5 0.7 slice-start.1
  35.5 25.7 %copy-start.10 = (bf16[256,1024]{1,0:T(8,128)(2,1)S(1)}, bf16[256,1024]{1,0:T(8,128)(2,1)}, u32[]{:S(2)}) copy-start(bf16[256,1024]{1,0:T(8,128)(2,1)} %param.20) | copy-start | bytes 1572868
  50.0 0.9 %copy-start.3 = (bf16[256,256]{1,0:T(8,128)(2,1)S(1)}, bf16[256,256]{1,0:T(8,128)(2,1)}, u32[]{:S(2)}) copy-start(bf16[256,256]{1,0:T(8,128)(2,1)} %param.17) | copy-start | bytes 393220
  50.3 0.7 %copy-start.8 = (bf16[1,8,1024]{2,1,0:T(8,128)(2,1)S(1)}, bf16[1,8,1024]{2,1,0:T(8,128)(2,1)}, u32[]{:S(2)}) copy-start(bf16[1,8,1024]{2,1,0:T(8,128)(2,1)} %copy-done.7) | copy-start | bytes 49156
  53.1 7.9 %all-to-all-start = ((bf16[8,2,128]{2,1,0:T(2,128)(2,1)}), bf16[8,2,128]{2,1,0:T(2,128)(2,1)S(1)}, u32[]{:S(2)}, u32[]{:S(2)}) async-start(bf16[8,2,128]{2,1,0:T(2,128)(2,1)} %reshape.228), calls=%async_computation | async-start | bytes 8192 | tf_op jit(solution)/shard_map/all_to_all | solution.py:148
  61.3 1.1 %copy-start.4 = (bf16[256,256]{1,0:T(8,128)(2,1)S(1)}, bf16[256,256]{1,0:T(8,128)(2,1)}, u32[]{:S(2)}) copy-start(bf16[256,256]{1,0:T(8,128)(2,1)} %param.21) | copy-start | bytes 393220
  61.3 1.6 %copy-start.2 = (bf16[256,1024]{1,0:T(8,128)(2,1)S(1)}, bf16[256,1024]{1,0:T(8,128)(2,1)}, u32[]{:S(2)}) copy-start(bf16[256,1024]{1,0:T(8,128)(2,1)} %param.22) | copy-start | bytes 1572868
  61.5 1.3 %copy-start.1 = (bf16[1024,256]{1,0:T(8,128)(2,1)S(1)}, bf16[1024,256]{1,0:T(8,128)(2,1)}, u32[]{:S(2)}) copy-start(bf16[1024,256]{1,0:T(8,128)(2,1)} %param.23) | copy-start | bytes 1572868
where the time goes:
time: 72.2 us; the launch traced here: 71.7 us
  blocking collectives  41.9 us (58%)
  local copies, waits for them, and re-layouts  9.98 us (14%)
  starting transfers between devices  8.51 us (12%)
  waiting for transfers between devices  4.3 us (6%)
  other arithmetic  3.88 us (5%)
  matrix products  2.23 us (3%)
  between operations  0.87 us (1%)
    all_gather x1, blocking collectives, body(): lax.all_gather(projected[..., expanded_dimension:3 * expanded_dimension],...  13.4 us
    unnamed x1, blocking collectives  11.7 us
    all_gather x1, blocking collectives, body(): pair_bias = lax.all_gather(local_bias, 'dap', axis=2, tiled=True)  9.75 us
    all_to_all x1, blocking collectives, body(): lax.all_to_all(mixed, 'dap', split_axis=0, concat_axis=1, tiled=True)  7.05 us
    unnamed x37, local copies, waits for them, and re-layouts  7.04 us
    all_to_all x1, starting transfers between devices, body(): lax.all_to_all(keep_blocks, 'dap', split_axis=1, concat_axis=0, tiled=True)  5.2 us
    all_to_all x1, waiting for transfers between devices, body(): lax.all_to_all(blocks, 'dap', split_axis=1, concat_axis=0, tiled=True)  4.3 us
    all_to_all x1, starting transfers between devices, body(): lax.all_to_all(blocks, 'dap', split_axis=1, concat_axis=0, tiled=True)  3.31 us
  transfers between devices with their start and end apart: 2, of which 1 were waited for; matrix products, arithmetic and copies ran while one was open for 8% of the time, Pallas kernels for 0%

commit v1 on v0

--- a/solution.py
+++ b/solution.py
@@ -6,6 +6,18 @@
 HEAD_TOTAL = 8
 HEAD_DEPTH = 32
 epsilon = 1e-05
+
+
+def split_up(array, dim, size):
+    shape = array.shape
+    blocks = array.reshape(*shape[:dim], size, shape[dim] // size, *shape[dim + 1 :])
+    return jnp.moveaxis(blocks, dim, 0)
+
+
+def laid_out(blocks, dim):
+    blocks = jnp.moveaxis(blocks, 0, dim)
+    shape = blocks.shape
+    return blocks.reshape(*shape[:dim], shape[dim] * shape[dim + 1], *shape[dim + 2 :])
 
 
 def layer_norm(inputs):
@@ -150,7 +162,15 @@
     inputs_col = (jnp.moveaxis(column_block[:, 0], 1, 0), jnp.moveaxis(column_keep[:, 0], 1, 0))
     output_list = lax.map(single_column, inputs_col)
     mixed = jnp.moveaxis(output_list, 0, 1)[:, None]
-    returned = lax.all_to_all(mixed, "dap", split_axis=0, concat_axis=1, tiled=True)
+    size, here = (lax.axis_size("dap"), lax.axis_index("dap"))
+    pieces = split_up(mixed, 0, size)
+    result = pieces
+    for step in range(1, size):
+        target, source = ((here + step) % size, (here - step) % size)
+        sent = lax.dynamic_index_in_dim(pieces, target, 0)
+        received = lax.ppermute(sent, "dap", [(i, (i + step) % size) for i in range(size)])
+        result = lax.dynamic_update_slice_in_dim(result, received, source, axis=0)
+    returned = laid_out(result, 1)
     return returned.reshape(row_count, local_residues, channels)
 
 

time: 72.2 us -> 74 us (1.025)
  blocking collectives: 41.9 us -> 34.8 us
  starting transfers between devices: 8.51 us -> 15.5 us
  waiting for transfers between devices: 4.3 us -> 5.81 us
  local copies, waits for them, and re-layouts: 9.98 us -> 10.8 us
  other arithmetic: 3.88 us -> 3.13 us
    all_to_all x1 -> x0, blocking collectives: 7.05 us -> none  [body(): lax.all_to_all(mixed, 'dap', split_axis=0, concat_axis=1, tiled=True)]
    ppermute x0 -> x7, starting transfers between devices: none -> 6.99 us  [body(): lax.ppermute(sent, 'dap', [(i, (i + step) % size) for i in range(size)])]
    ppermute x0 -> x7, waiting for transfers between devices: none -> 1.5 us  [body(): lax.ppermute(sent, 'dap', [(i, (i + step) % size) for i in range(size)])]
    dynamic_update_slice x0 -> x7, local copies, waits for them, and re-layouts: none -> 1.5 us  [body(): result = lax.dynamic_update_slice_in_dim(result, received, source, axis=0)]
    unnamed x37 -> x36, local copies, waits for them, and re-layouts: 7.04 us -> 6.35 us
  transfers between devices with their start and end apart: 2 -> 9, of which waited for: 1 -> 3; matrix products, arithmetic and copies ran while one was open for 8% -> 8% of each run, Pallas kernels for 0% -> 0%
where the time goes in v1:
time: 74 us; the launch traced here: 73.2 us
  blocking collectives  34.8 us (47%)
  starting transfers between devices  15.5 us (21%)
  local copies, waits for them, and re-layouts  10.8 us (15%)
  waiting for transfers between devices  5.81 us (8%)
  other arithmetic  3.13 us (4%)
  matrix products  2.23 us (3%)
  between operations  0.92 us (1%)
    all_gather x1, blocking collectives, body(): lax.all_gather(projected[..., expanded_dimension:3 * expanded_dimension],...  13.4 us
    unnamed x1, blocking collectives  11.7 us
    all_gather x1, blocking collectives, body(): pair_bias = lax.all_gather(local_bias, 'dap', axis=2, tiled=True)  9.75 us
    ppermute x7, starting transfers between devices, body(): lax.ppermute(sent, 'dap', [(i, (i + step) % size) for i in range(size)])  6.99 us
    unnamed x36, local copies, waits for them, and re-layouts  6.35 us
    all_to_all x1, starting transfers between devices, body(): lax.all_to_all(keep_blocks, 'dap', split_axis=1, concat_axis=0, tiled=True)  5.2 us
    all_to_all x1, waiting for transfers between devices, body(): lax.all_to_all(blocks, 'dap', split_axis=1, concat_axis=0, tiled=True)  4.3 us
    all_to_all x1, starting transfers between devices, body(): lax.all_to_all(blocks, 'dap', split_axis=1, concat_axis=0, tiled=True)  3.31 us
  transfers between devices with their start and end apart: 9, of which 3 were waited for; matrix products, arithmetic and copies ran while one was open for 8% of the time, Pallas kernels for 0%

profile of v1, /device:TPU:0, one launch (start us, length us, event | category | flops | bytes accessed | tf_op | source)
XLA Modules:
  0.0 73.2 jit_solution(17179305332908810068)
XLA Ops:
  0.0 0.7 convert_bitcast_fusion.1
  0.7 0.7 copy.48
  1.4 5.2 %all-to-all-start.1 = ((bf16[1,8,1]{2,0,1:T(2,128)(2,1)}), bf16[1,8,1]{2,0,1:T(2,128)(2,1)S(1)}, u32[]{:S(2)}, u32[]{:S(2)}) async-start(bf16[1,8,1]{2,0,1:T(2,128)(2,1)} %copy.48), calls=%async_computation.1 | async-start | bytes 8192 | tf_op jit(solution)/shard_map/all_to_all | solution.py:161
  6.6 0.7 copy-done.13
  7.3 0.1 dynamic_slice.57
  7.4 0.1 broadcast_subtract_fusion
  7.6 0.5 copy-done.6
  8.0 0.1 convert_reduce_fusion.1
  8.1 0.2 fusion.37
  8.3 0.2 fusion.12
  8.6 0.6 copy-done.7
  9.2 0.7 copy-done.5
  9.9 0.1 convert_reduce_fusion
  10.0 0.2 fusion.23
  10.1 0.1 fusion.21
  10.2 0.6 copy-done.10
  10.8 0.7 copy-done.12
  11.5 0.1 fusion.13
  11.6 0.1 copy.42
  11.7 9.7 %all_gather.11 = bf16[8,8,32]{1,0,2:T(8,128)(2,1)S(1)} all-gather(bf16[8,8,4]{1,0,2:T(8,128)(2,1)S(1)} %copy.42), channel_id=1, replica_groups=mesh['dap'=8,'seq'=4] {'dap'}, dimensions={2}, use_global_device_ids=true | all-gather | bytes 4608 | tf_op jit(solution)/shard_map/all_gather | solution.py:108
  21.5 0.1 copy.43
  21.6 0.6 slice-done
  22.2 13.4 %all_gather.9 = bf16[1,32,512]{2,1,0:T(8,128)(2,1)S(1)} all-gather(bf16[1,8,512]{2,1,0:T(8,128)(2,1)S(1)} %slice-done), channel_id=1, replica_groups=mesh['dap'=8,'seq'=4] {'seq'}, dimensions={1}, use_global_device_ids=true | all-gather | bytes 40960 | tf_op jit(solution)/shard_map/all_gather | solution.py:120
  35.6 0.1 reshape.223
  35.7 0.6 slice-done.1
  36.2 0.1 reshape.222
  36.3 0.6 dynamic-slice.7
  37.6 0.2 dynamic-update-slice
  37.8 11.7 %all-reduce = bf16[32]{0:T(256)(128)(2,1)S(1)} all-reduce(bf16[32]{0:T(256)(128)(2,1)S(1)} %dynamic-update-slice), channel_id=1, replica_groups=mesh['dap'=8,'seq'=4] {'seq'}, use_global_device_ids=true, to_apply=%add | all-reduce | flops 32 | bytes 128
  49.5 0.1 fusion.8
  49.7 0.2 fusion.72
  49.9 0.1 reshape.221
  50.0 0.3 convolution_bitcast_fusion.1
  50.3 0.1 broadcast_in_dim.72
  50.3 0.5 copy-done.3
  50.9 0.1 copy-done.8
  51.0 0.1 fusion.18
  51.2 0.5 broadcast.234
  51.7 0.7 reduce.5
  52.3 0.6 reshape.242
  53.0 3.3 %all-to-all-start = ((bf16[8,2,128]{2,1,0:T(2,128)(2,1)}), bf16[8,2,128]{2,1,0:T(2,128)(2,1)S(1)}, u32[]{:S(2)}, u32[]{:S(2)}) async-start(bf16[8,2,128]{2,1,0:T(2,128)(2,1)} %reshape.242), calls=%async_computation | async-start | bytes 8192 | tf_op jit(solution)/shard_map/all_to_all | solution.py:160
  56.3 0.2 compare_reduce_fusion
  56.5 4.3 %all-to-all-done = bf16[8,2,128]{2,1,0:T(2,128)(2,1)S(1)} async-done(((bf16[8,2,128]{2,1,0:T(2,128)(2,1)}), bf16[8,2,128]{2,1,0:T(2,128)(2,1)S(1)}, u32[]{:S(2)}, u32[]{:S(2)}) %all-to-all-start) | async-done | bytes 4128 | tf_op jit(solution)/shard_map/all_to_all | solution.py:160
  60.8 0.1 convert_reduce_fusion.2
  61.0 0.2 fusion.39
  61.2 0.2 convolution_convert_fusion
  61.4 0.1 reshape.229
  61.5 0.1 reshape.230
  61.6 0.1 fusion.6
  61.7 0.2 fusion.73
  61.9 0.1 reshape.227
  62.0 0.2 convolution_bitcast_fusion
  62.2 0.1 reshape.231
  62.3 0.3 fusion.78
  62.5 0.2 multiply_reduce_fusion
  62.7 0.4 fusion.17
  63.3 0.6 collective-permute-start.1
  63.9 1.4 %collective-permute-start.2 = (bf16[1,1,1,1,256]{4,3,2,1,0:T(2,128)(2,1)S(1)}, bf16[1,1,1,1,256]{4,3,2,1,0:T(2,128)(2,1)S(1)}, u32[]{:S(2)}, u32[]{:S(2)}) collective-permute-start(bf16[1,1,1,1,256]{4,3,2,1,0:T(2,128)(2,1)S(1)} %get-tuple-element.56), channel_id=1, source_target_pairs={{0,12},{4,16},{8,20},{12,24},{16,28},{20,0},{24,4},{28,8},{1,13},{... | collective-permute-start | bytes 1544 | tf_op jit(solution)/shard_map/ppermute | solution.py:171
  65.2 1.5 %collective-permute-start.3 = (bf16[1,1,1,1,256]{4,3,2,1,0:T(2,128)(2,1)S(1)}, bf16[1,1,1,1,256]{4,3,2,1,0:T(2,128)(2,1)S(1)}, u32[]{:S(2)}, u32[]{:S(2)}) collective-permute-start(bf16[1,1,1,1,256]{4,3,2,1,0:T(2,128)(2,1)S(1)} %get-tuple-element.47), channel_id=1, source_target_pairs={{0,16},{4,20},{8,24},{12,28},{16,0},{20,4},{24,8},{28,12},{1,17},{... | collective-permute-start | bytes 1544 | tf_op jit(solution)/shard_map/ppermute | solution.py:171
  66.7 0.4 collective-permute-done
  67.1 2.0 %collective-permute-start.5 = (bf16[1,1,1,1,256]{4,3,2,1,0:T(2,128)(2,1)S(1)}, bf16[1,1,1,1,256]{4,3,2,1,0:T(2,128)(2,1)S(1)}, u32[]{:S(2)}, u32[]{:S(2)}) collective-permute-start(bf16[1,1,1,1,256]{4,3,2,1,0:T(2,128)(2,1)S(1)} %get-tuple-element.45), channel_id=1, source_target_pairs={{0,24},{4,28},{8,0},{12,4},{16,8},{20,12},{24,16},{28,20},{1,25},{... | collective-permute-start | bytes 1544 | tf_op jit(solution)/shard_map/ppermute | solution.py:171
  69.1 1.5 %collective-permute-start.6 = (bf16[1,1,1,1,256]{4,3,2,1,0:T(2,128)(2,1)S(1)}, bf16[1,1,1,1,256]{4,3,2,1,0:T(2,128)(2,1)S(1)}, u32[]{:S(2)}, u32[]{:S(2)}) collective-permute-start(bf16[1,1,1,1,256]{4,3,2,1,0:T(2,128)(2,1)S(1)} %get-tuple-element.44), channel_id=1, source_target_pairs={{0,28},{4,0},{8,4},{12,8},{16,12},{20,16},{24,20},{28,24},{1,29},{... | collective-permute-start | bytes 1544 | tf_op jit(solution)/shard_map/ppermute | solution.py:171
  70.8 1.1 %collective-permute-done.6 = bf16[1,1,1,1,256]{4,3,2,1,0:T(2,128)(2,1)S(1)} collective-permute-done((bf16[1,1,1,1,256]{4,3,2,1,0:T(2,128)(2,1)S(1)}, bf16[1,1,1,1,256]{4,3,2,1,0:T(2,128)(2,1)S(1)}, u32[]{:S(2)}, u32[]{:S(2)}) %collective-permute-start.6) | collective-permute-done | bytes 544 | tf_op jit(solution)/shard_map/ppermute | solution.py:171
  71.9 1.3 %dynamic_update_slice.40 = bf16[1,8,256]{2,1,0:T(8,128)(2,1)} dynamic-update-slice(bf16[1,8,256]{2,1,0:T(8,128)(2,1)} %copy-done.9, bf16[1,1,256]{2,1,0:T(2,128)(2,1)S(1)} %bitcast.98, s32[]{:T(128)} %constant.190.clone.1, s32[]{:T(128)S(6)} %select_n.149, s32[]{:T(128)} %constant.190.clone.1) | dynamic-update-slice | bytes 1028 | tf_op jit(solution)/shard_map/dynamic_update_slice | solution.py:172
  (58 shorter events, 0.6 us)
Async XLA Ops:
  0.0 8.3 %copy-start = (bf16[256,1024]{1,0:T(8,128)(2,1)S(1)}, bf16[256,1024]{1,0:T(8,128)(2,1)}, u32[]{:S(2)}) copy-start(bf16[256,1024]{1,0:T(8,128)(2,1)} %param.16) | copy-start | bytes 1572868
  1.4 51.5 %all-to-all-start.1 = ((bf16[1,8,1]{2,0,1:T(2,128)(2,1)}), bf16[1,8,1]{2,0,1:T(2,128)(2,1)S(1)}, u32[]{:S(2)}, u32[]{:S(2)}) async-start(bf16[1,8,1]{2,0,1:T(2,128)(2,1)} %copy.48), calls=%async_computation.1 | async-start | bytes 8192 | tf_op jit(solution)/shard_map/all_to_all | solution.py:161
  6.6 0.7 copy-start.13
  7.3 0.7 copy-start.6
  8.6 0.6 copy-start.7
  9.2 0.7 copy-start.5
  10.1 0.7 copy-start.10
  10.8 0.7 copy-start.12
  21.5 0.7 slice-start
  35.5 0.8 %copy-start.14 = (u32[32]{0:T(128)S(1)}, u32[32]{0:T(128)}, u32[]{:S(2)}) copy-start(u32[32]{0:T(128)} %constant.215) | copy-start | bytes 388
  35.5 0.7 slice-start.1
  35.5 25.6 %copy-start.11 = (bf16[256,1024]{1,0:T(8,128)(2,1)S(1)}, bf16[256,1024]{1,0:T(8,128)(2,1)}, u32[]{:S(2)}) copy-start(bf16[256,1024]{1,0:T(8,128)(2,1)} %param.20) | copy-start | bytes 1572868
  50.0 0.9 %copy-start.3 = (bf16[256,256]{1,0:T(8,128)(2,1)S(1)}, bf16[256,256]{1,0:T(8,128)(2,1)}, u32[]{:S(2)}) copy-start(bf16[256,256]{1,0:T(8,128)(2,1)} %param.17) | copy-start | bytes 393220
  50.3 0.7 %copy-start.8 = (bf16[1,8,1024]{2,1,0:T(8,128)(2,1)S(1)}, bf16[1,8,1024]{2,1,0:T(8,128)(2,1)}, u32[]{:S(2)}) copy-start(bf16[1,8,1024]{2,1,0:T(8,128)(2,1)} %copy-done.7) | copy-start | bytes 49156
  53.0 7.9 %all-to-all-start = ((bf16[8,2,128]{2,1,0:T(2,128)(2,1)}), bf16[8,2,128]{2,1,0:T(2,128)(2,1)S(1)}, u32[]{:S(2)}, u32[]{:S(2)}) async-start(bf16[8,2,128]{2,1,0:T(2,128)(2,1)} %reshape.242), calls=%async_computation | async-start | bytes 8192 | tf_op jit(solution)/shard_map/all_to_all | solution.py:160
  61.2 1.1 %copy-start.4 = (bf16[256,256]{1,0:T(8,128)(2,1)S(1)}, bf16[256,256]{1,0:T(8,128)(2,1)}, u32[]{:S(2)}) copy-start(bf16[256,256]{1,0:T(8,128)(2,1)} %param.21) | copy-start | bytes 393220
  61.2 1.6 %copy-start.2 = (bf16[256,1024]{1,0:T(8,128)(2,1)S(1)}, bf16[256,1024]{1,0:T(8,128)(2,1)}, u32[]{:S(2)}) copy-start(bf16[256,1024]{1,0:T(8,128)(2,1)} %param.22) | copy-start | bytes 1572868
  61.4 1.3 %copy-start.1 = (bf16[1024,256]{1,0:T(8,128)(2,1)S(1)}, bf16[1024,256]{1,0:T(8,128)(2,1)}, u32[]{:S(2)}) copy-start(bf16[1024,256]{1,0:T(8,128)(2,1)} %param.23) | copy-start | bytes 1572868
  63.2 4.0 %collective-permute-start = (bf16[1,1,1,1,256]{4,3,2,1,0:T(2,128)(2,1)S(1)}, bf16[1,1,1,1,256]{4,3,2,1,0:T(2,128)(2,1)S(1)}, u32[]{:S(2)}, u32[]{:S(2)}) collective-permute-start(bf16[1,1,1,1,256]{4,3,2,1,0:T(2,128)(2,1)S(1)} %get-tuple-element.60), channel_id=1, source_target_pairs={{0,4},{4,8},{8,12},{12,16},{16,20},{20,24},{24,28},{28,0},{1,5},{5... | collective-permute-start | bytes 1544 | tf_op jit(solution)/shard_map/ppermute | solution.py:171
  63.3 5.9 %collective-permute-start.1 = (bf16[1,1,1,1,256]{4,3,2,1,0:T(2,128)(2,1)S(1)}, bf16[1,1,1,1,256]{4,3,2,1,0:T(2,128)(2,1)S(1)}, u32[]{:S(2)}, u32[]{:S(2)}) collective-permute-start(bf16[1,1,1,1,256]{4,3,2,1,0:T(2,128)(2,1)S(1)} %get-tuple-element.58), channel_id=1, source_target_pairs={{0,8},{4,12},{8,16},{12,20},{16,24},{20,28},{24,0},{28,4},{1,9},{5... | collective-permute-start | bytes 1544 | tf_op jit(solution)/shard_map/ppermute | solution.py:171
  63.9 6.8 %collective-permute-start.2 = (bf16[1,1,1,1,256]{4,3,2,1,0:T(2,128)(2,1)S(1)}, bf16[1,1,1,1,256]{4,3,2,1,0:T(2,128)(2,1)S(1)}, u32[]{:S(2)}, u32[]{:S(2)}) collective-permute-start(bf16[1,1,1,1,256]{4,3,2,1,0:T(2,128)(2,1)S(1)} %get-tuple-element.56), channel_id=1, source_target_pairs={{0,12},{4,16},{8,20},{12,24},{16,28},{20,0},{24,4},{28,8},{1,13},{... | collective-permute-start | bytes 1544 | tf_op jit(solution)/shard_map/ppermute | solution.py:171
  65.2 5.5 %collective-permute-start.3 = (bf16[1,1,1,1,256]{4,3,2,1,0:T(2,128)(2,1)S(1)}, bf16[1,1,1,1,256]{4,3,2,1,0:T(2,128)(2,1)S(1)}, u32[]{:S(2)}, u32[]{:S(2)}) collective-permute-start(bf16[1,1,1,1,256]{4,3,2,1,0:T(2,128)(2,1)S(1)} %get-tuple-element.47), channel_id=1, source_target_pairs={{0,16},{4,20},{8,24},{12,28},{16,0},{20,4},{24,8},{28,12},{1,17},{... | collective-permute-start | bytes 1544 | tf_op jit(solution)/shard_map/ppermute | solution.py:171
  66.7 4.0 %collective-permute-start.4 = (bf16[1,1,1,1,256]{4,3,2,1,0:T(2,128)(2,1)S(1)}, bf16[1,1,1,1,256]{4,3,2,1,0:T(2,128)(2,1)S(1)}, u32[]{:S(2)}, u32[]{:S(2)}) collective-permute-start(bf16[1,1,1,1,256]{4,3,2,1,0:T(2,128)(2,1)S(1)} %get-tuple-element.46), channel_id=1, source_target_pairs={{0,20},{4,24},{8,28},{12,0},{16,4},{20,8},{24,12},{28,16},{1,21},{... | collective-permute-start | bytes 1544 | tf_op jit(solution)/shard_map/ppermute | solution.py:171
  67.1 3.7 %collective-permute-start.5 = (bf16[1,1,1,1,256]{4,3,2,1,0:T(2,128)(2,1)S(1)}, bf16[1,1,1,1,256]{4,3,2,1,0:T(2,128)(2,1)S(1)}, u32[]{:S(2)}, u32[]{:S(2)}) collective-permute-start(bf16[1,1,1,1,256]{4,3,2,1,0:T(2,128)(2,1)S(1)} %get-tuple-element.45), channel_id=1, source_target_pairs={{0,24},{4,28},{8,0},{12,4},{16,8},{20,12},{24,16},{28,20},{1,25},{... | collective-permute-start | bytes 1544 | tf_op jit(solution)/shard_map/ppermute | solution.py:171
  69.1 2.8 %collective-permute-start.6 = (bf16[1,1,1,1,256]{4,3,2,1,0:T(2,128)(2,1)S(1)}, bf16[1,1,1,1,256]{4,3,2,1,0:T(2,128)(2,1)S(1)}, u32[]{:S(2)}, u32[]{:S(2)}) collective-permute-start(bf16[1,1,1,1,256]{4,3,2,1,0:T(2,128)(2,1)S(1)} %get-tuple-element.44), channel_id=1, source_target_pairs={{0,28},{4,0},{8,4},{12,8},{16,12},{20,16},{24,20},{28,24},{1,29},{... | collective-permute-start | bytes 1544 | tf_op jit(solution)/shard_map/ppermute | solution.py:171
  70.8 1.1 %copy-start.9 = (bf16[1,8,256]{2,1,0:T(8,128)(2,1)}, bf16[1,8,256]{2,1,0:T(8,128)(2,1)S(1)}, u32[]{:S(2)}) copy-start(bf16[1,8,256]{2,1,0:T(8,128)(2,1)S(1)} %dynamic_update_slice.39) | copy-start | bytes 12292
